TPU v7x, 32 devices: a whole 2x2x4 slice. The times are simulated.
32 devices in a mesh: dp: 2 (over x), expert: 16 (over z, y, core).
Axes of the slice: x: 2, y: 2, z: 4, core: 2. Of those that a mesh axis runs over, the one named last changes fastest.
Arguments:
- q_latent: bfloat16 [128, 16, 576], P(('expert', 'dp')), may hold values from -48 to 48
- latent_cache: bfloat16 [128, 512, 576], P(('expert', 'dp')), may hold values from -10 to 10
- lengths: int32 [128], P(('expert', 'dp')), may hold values from 2 to 512
- residual: bfloat16 [128, 2048], P(('expert', 'dp')), may hold values from -6 to 6
- adapter_ids: int32 [128], P(('expert', 'dp')), may hold values from 0 to 31
- value_out: bfloat16 [8192, 2048], P('expert'), may hold values from -0.0625 to 0.0625
- adapter_down: bfloat16 [8192, 512], P('expert'), may hold values from -0.0625 to 0.0625
- adapter_up_factors: bfloat16 [512, 2048], P('expert'), may hold values from -1.5 to 1.5
- norm_gain: bfloat16 [2048], replicated, may hold values from 0.099609375 to 1.8984375
- expert_ids: int32 [128, 6], P('expert'), may hold values from 0 to 15, all different within a row; in each aligned block of 8 rows (0 to 7, 8 to 15, ...) at most 6 rows name the same one
- gate_weights: float32 [128, 6], P('expert'), may hold values from 0.05 to 0.5
- w_gate: bfloat16 [16, 2048, 1024], P('expert', None, 'dp'), may hold values from -0.125 to 0.125
- w_up: bfloat16 [16, 2048, 1024], P('expert', None, 'dp'), may hold values from -0.125 to 0.125
- w_down: bfloat16 [16, 2048, 1024], P('expert', None, 'dp'), may hold values from -0.1875 to 0.1875
Outputs:
- layer_out: bfloat16 [128, 2048], P(('expert', 'dp'))
Inputs may be any that keep to these rules, and one draw needn't show every extreme that they name: `expert_ids`: each row names 6 different experts. Requests e * 8 to e * 8 + 7 form aligned blocks; in each block no expert is named by more than 6 rows, and in some block an expert is named by exactly 6 rows.
All inputs are finite; a program needn't handle non-finite values.
Results may differ from a plain program's by a relative error of at most 0.008.
Values may be sent and summed in bfloat16 or wider, within the bound.
A program may use at most 64 MiB of HBM per device.

v0:
```python
import jax
import jax.numpy as jnp
from jax import lax
from jax.sharding import PartitionSpec as P

LAT = 512
ADAPTER_RANK = 16
SOFTMAX_SCALE = 192.0 ** (-0.5)
ADAPTER_SCALE = 2.0
EPSILON = 1e-06


def attend_one(query, latent_rows, length):
    scores = (
        lax.dot_general(
            query, latent_rows, (((1,), (1,)), ((), ())), preferred_element_type=jnp.float32
        )
        * SOFTMAX_SCALE
    )
    valid_mask = jnp.arange(latent_rows.shape[0], dtype=jnp.int32) < length
    scores = jnp.where(valid_mask[None, :], scores, -1e30)
    row_max = jnp.max(scores, axis=1, keepdims=True)
    raised = jnp.exp(scores - row_max)
    weights_bf = (raised / jnp.sum(raised, axis=1, keepdims=True)).astype(jnp.bfloat16)
    return jnp.dot(weights_bf, latent_rows[:, :LAT], preferred_element_type=jnp.float32).astype(
        jnp.bfloat16
    )


def expert_rows(tokens, gate_part, up_part, down_part):
    gate_act = jnp.dot(tokens, gate_part, preferred_element_type=jnp.float32)
    up_act = jnp.dot(tokens, up_part, preferred_element_type=jnp.float32)
    hidden_bf = (jax.nn.silu(gate_act) * up_act).astype(jnp.bfloat16)
    return lax.dot_general(
        hidden_bf, down_part, (((1,), (1,)), ((), ())), preferred_element_type=jnp.float32
    )


def local(
    q_latent,
    latent_cache,
    lengths,
    residual,
    adapter_ids,
    value_out,
    adapter_down,
    adapter_up_factors,
    norm_gain,
    expert_ids,
    gate_weights,
    w_gate,
    w_up,
    w_down,
):
    requests = residual.shape[0]
    model_width = residual.shape[1]
    head_count = q_latent.shape[1]
    latent_out = jax.vmap(attend_one)(q_latent, latent_cache, lengths).reshape(
        requests, head_count * LAT
    )
    pieces = lax.all_to_all(latent_out, "expert", split_axis=1, concat_axis=0, tiled=True)
    group_ids = lax.all_gather(adapter_ids, "expert", axis=0, tiled=True)
    group_rows = pieces.shape[0]
    adapters = adapter_down.shape[1] // ADAPTER_RANK
    owned_count = adapter_up_factors.shape[0] // ADAPTER_RANK
    down_projected_rows = jnp.dot(pieces, adapter_down, preferred_element_type=jnp.float32).reshape(
        group_rows, adapters, ADAPTER_RANK
    )
    chosen_adapters = group_ids[:, None] == jnp.arange(adapters, dtype=jnp.int32)[None, :]
    adapter_output = jnp.sum(
        jnp.where(chosen_adapters[:, :, None], down_projected_rows, 0.0), axis=1
    )
    adapter_down_rows = lax.psum(adapter_output, "expert")
    adapter_scaled_output = (ADAPTER_SCALE * adapter_down_rows).astype(jnp.bfloat16)
    first_owned = lax.axis_index("expert") * owned_count
    holder_mask = (
        group_ids[:, None] == first_owned + jnp.arange(owned_count, dtype=jnp.int32)[None, :]
    )
    spread_rows = jnp.where(
        holder_mask[:, :, None], adapter_scaled_output[:, None, :], jnp.zeros((), jnp.bfloat16)
    ).reshape(group_rows, owned_count * ADAPTER_RANK)
    attention = lax.psum_scatter(
        jnp.dot(pieces, value_out, preferred_element_type=jnp.float32)
        + jnp.dot(spread_rows, adapter_up_factors, preferred_element_type=jnp.float32),
        "expert",
        scatter_dimension=0,
        tiled=True,
    )
    residual_flow = residual.astype(jnp.float32) + attention
    inverse_rms = lax.rsqrt(
        jnp.mean(residual_flow * residual_flow, axis=1, keepdims=True) + EPSILON
    )
    normed = (residual_flow * inverse_rms * norm_gain.astype(jnp.float32)).astype(jnp.bfloat16)
    column = lax.all_gather(normed, "dp", axis=0, tiled=True)
    tokens = column.shape[0]
    top_count = expert_ids.shape[1]
    experts = lax.axis_size("expert") * w_gate.shape[0]
    share_size = max(1, 2 * requests * top_count // experts)
    dp_count = lax.axis_size("dp")
    slot_count = share_size * dp_count
    member = expert_ids[:, :, None] == jnp.arange(experts, dtype=jnp.int32)[None, None, :]
    flat_hits = member.reshape(tokens * top_count, experts).astype(jnp.int32)
    slot_rank = jnp.sum((jnp.cumsum(flat_hits, axis=0) - 1) * flat_hits, axis=1).reshape(
        tokens, top_count
    )
    placed = member[:, :, :, None] & (
        slot_rank[:, :, None, None] == jnp.arange(slot_count, dtype=jnp.int32)[None, None, None, :]
    )
    routing = jnp.any(placed, axis=1).reshape(tokens, experts * slot_count)
    combine = jnp.sum(jnp.where(placed, gate_weights[:, :, None, None], 0.0), axis=1).reshape(
        tokens, experts * slot_count
    )
    routing_rows = routing.T.astype(jnp.bfloat16)
    outgoing = (
        jnp.dot(routing_rows, column, preferred_element_type=jnp.float32)
        .astype(jnp.bfloat16)
        .reshape(experts, slot_count, model_width)
    )
    arrived = lax.all_to_all(outgoing, "expert", split_axis=0, concat_axis=0, tiled=True)
    produced = expert_rows(arrived.reshape(-1, model_width), w_gate[0], w_up[0], w_down[0])
    partial_value = produced.reshape(arrived.shape[0], arrived.shape[1], model_width)
    returned = lax.all_to_all(
        partial_value.astype(jnp.bfloat16), "expert", split_axis=0, concat_axis=0, tiled=True
    ).astype(partial_value.dtype)
    routed_column = jnp.dot(
        combine,
        returned.reshape(experts * slot_count, model_width),
        precision=lax.Precision.HIGHEST,
        preferred_element_type=jnp.float32,
    )
    routed_sum = lax.psum_scatter(
        routed_column.astype(jnp.bfloat16), "dp", scatter_dimension=0, tiled=True
    ).astype(jnp.float32)
    return (residual_flow + routed_sum).astype(jnp.bfloat16)


def solution(mesh):
    in_specs = (
        P(("expert", "dp"), None, None),
        P(("expert", "dp"), None, None),
        P(("expert", "dp")),
        P(("expert", "dp"), None),
        P(("expert", "dp")),
        P("expert", None),
        P("expert", None),
        P("expert", None),
        P(),
        P("expert", None),
        P("expert", None),
        P("expert", None, "dp"),
        P("expert", None, "dp"),
        P("expert", None, "dp"),
    )
    out_specs = P(("expert", "dp"), None)
    return jax.shard_map(local, mesh=mesh, in_specs=in_specs, out_specs=out_specs, check_vma=False)
```

profile of v0, /device:TPU:0, one launch (start us, length us, event | category | flops | bytes accessed | tf_op | source)
XLA Modules:
  0.0 223.4 jit_solution(10527450560244738211)
XLA Ops:
  6.5 0.9 iota_compare_fusion.4
  7.4 2.1 fusion.17
  9.8 2.3 %fusion.19 = bf16[4,16,512]{2,1,0:T(8,128)(2,1)S(1)} fusion(bf16[4,512,576]{1,2,0:T(8,128)(2,1)} %param.15, f32[4,16]{1,0:T(4,128)S(1)} %fusion.31, f32[4,16,512]{2,1,0:T(8,128)S(1)} %fusion.17), kind=kOutput, calls=%fused_computation.21 | convolution fusion | flops 33686080 | bytes 2426880 | tf_op jit(solution)/shard_map/vmap()/dot_general | solution.py:25
  12.1 0.7 copy.29
  12.8 7.4 %all-to-all-start = ((bf16[4,16,512]{2,0,1:T(4,128)(2,1)}), bf16[4,16,512]{2,0,1:T(4,128)(2,1)S(1)}, u32[]{:S(2)}, u32[]{:S(2)}) async-start(bf16[4,16,512]{2,0,1:T(4,128)(2,1)} %copy.29), calls=%async_computation | async-start | bytes 131072 | tf_op jit(solution)/shard_map/all_to_all | solution.py:61
  20.4 0.6 fusion.30
  21.9 12.4 %all-reduce = s32[64]{0:T(128)S(1)} all-reduce(s32[64]{0:T(128)S(1)} %dynamic-update-slice), channel_id=1, replica_groups=mesh['dp'=2,'expert'=16] {'expert'}, use_global_device_ids=true, to_apply=%add | all-reduce | flops 64 | bytes 512
  35.7 30.0 %psum.7 = f32[64,16]{0,1:T(8,128)S(1)} all-reduce(f32[64,16]{0,1:T(8,128)S(1)} %fusion.16), channel_id=1, replica_groups=mesh['dp'=2,'expert'=16] {'expert'}, use_global_device_ids=true, to_apply=%region_3.4 | all-reduce | flops 1024 | bytes 8192 | tf_op jit(solution)/shard_map/psum | solution.py:73
  65.7 2.1 fusion.32
  67.8 1.1 convolution_add_fusion
  70.0 87.0 %all-reduce.5.cloned.1.call-done = f32[64,2048]{1,0:T(8,128)} async-done(((f32[64,2048]{1,0:T(8,128)}), f32[64,2048]{1,0:T(8,128)}) %all-reduce.5.cloned.1.call-update) | async-done | bytes 524304
  157.0 1.0 multiply_reduce_fusion
  158.0 0.9 fusion.28
  158.9 4.4 %all-gather = bf16[2,4,2048]{2,1,0:T(4,128)(2,1)S(1)} all-gather(bf16[1,4,2048]{2,1,0:T(4,128)(2,1)S(1)} %fusion.28), channel_id=1, replica_groups=mesh['dp'=2,'expert'=16] {'dp'}, dimensions={0}, use_global_device_ids=true | all-gather | bytes 49152 | tf_op jit(solution)/shard_map/all_gather | solution.py:94
  163.8 19.2 %all_to_all.26 = bf16[16,6,2048]{2,1,0:T(8,128)(2,1)S(1)} all-to-all(bf16[16,6,2048]{2,1,0:T(8,128)(2,1)S(1)} %reshape.122), channel_id=1, replica_groups=mesh['dp'=2,'expert'=16] {'expert'}, dimensions={0} | all-to-all | bytes 786432 | tf_op jit(solution)/shard_map/all_to_all | solution.py:119
  183.2 2.2 fusion.5
  186.0 0.8 convolution_convert_fusion
  186.7 1.0 copy.37
  187.8 4.2 %all-to-all-start.2 = ((bf16[16,6,2048]{2,1,0:T(8,128)(2,1)}), bf16[16,6,2048]{2,1,0:T(8,128)(2,1)S(1)}, u32[]{:S(2)}, u32[]{:S(2)}) async-start(bf16[16,6,2048]{2,1,0:T(8,128)(2,1)} %copy.37), calls=%async_computation.2 | async-start | bytes 1048576 | tf_op jit(solution)/shard_map/all_to_all | solution.py:122
  192.0 0.6 dynamic-slice.3
  193.4 12.8 %all-to-all-done.2 = bf16[16,6,2048]{2,1,0:T(8,128)(2,1)S(1)} async-done(((bf16[16,6,2048]{2,1,0:T(8,128)(2,1)}), bf16[16,6,2048]{2,1,0:T(8,128)(2,1)S(1)}, u32[]{:S(2)}, u32[]{:S(2)}) %all-to-all-start.2) | async-done | bytes 393248 | tf_op jit(solution)/shard_map/all_to_all | solution.py:122
  206.2 0.6 fusion.1
  206.8 8.3 %all-reduce.2 = bf16[8,2048]{1,0:T(8,128)(2,1)S(1)} all-reduce(bf16[8,2048]{1,0:T(8,128)(2,1)S(1)} %fusion.1), channel_id=3, replica_groups=mesh['dp'=2,'expert'=16] {'dp'}, use_global_device_ids=true, to_apply=%region_10.11.clone | all-reduce | flops 16384 | bytes 65536
  215.1 1.5 add_convert_fusion
  (59 shorter events, 3.8 us)
Async XLA Ops:
  6.5 179.4 %copy-start = (bf16[1,2048,512]{2,1,0:T(8,128)(2,1)S(1)}, bf16[1,2048,512]{2,1,0:T(8,128)(2,1)}, u32[]{:S(2)}) copy-start(bf16[1,2048,512]{2,1,0:T(8,128)(2,1)} %param.27) | copy-start | bytes 6291460
  9.6 10.7 %copy-start.4 = (s32[8,6]{1,0:T(8,128)S(1)}, s32[8,6]{1,0:T(8,128)}, u32[]{:S(2)}) copy-start(s32[8,6]{1,0:T(8,128)} %param.23) | copy-start | bytes 580
  9.6 10.8 %copy-start.7 = (u32[32]{0:T(128)S(1)}, u32[32]{0:T(128)}, u32[]{:S(2)}) copy-start(u32[32]{0:T(128)} %constant.49) | copy-start | bytes 388
  9.6 12.1 %copy-start.9 = (s32[4]{0:T(128)S(1)}, s32[4]{0:T(128)}, u32[]{:S(2)}) copy-start(s32[4]{0:T(128)} %param.18) | copy-start | bytes 52
  9.6 24.7 %copy-start.1 = (bf16[512,512]{1,0:T(8,128)(2,1)S(1)}, bf16[512,512]{1,0:T(8,128)(2,1)}, u32[]{:S(2)}) copy-start(bf16[512,512]{1,0:T(8,128)(2,1)} %param.20) | copy-start | bytes 1572868
  9.6 25.0 %copy-start.5 = (bf16[2048]{0:T(1024)(128)(2,1)S(1)}, bf16[2048]{0:T(1024)(128)(2,1)}, u32[]{:S(2)}) copy-start(bf16[2048]{0:T(1024)(128)(2,1)} %param.22) | copy-start | bytes 12292
  12.8 22.4 %all-to-all-start = ((bf16[4,16,512]{2,0,1:T(4,128)(2,1)}), bf16[4,16,512]{2,0,1:T(4,128)(2,1)S(1)}, u32[]{:S(2)}, u32[]{:S(2)}) async-start(bf16[4,16,512]{2,0,1:T(4,128)(2,1)} %copy.29), calls=%async_computation | async-start | bytes 131072 | tf_op jit(solution)/shard_map/all_to_all | solution.py:61
  20.2 136.8 %all-reduce.5.cloned.1.call-start = ((), (), s32[]{:S(2)}) async-start(), calls=%async_computation.3 | async-start | bytes 1048576
  34.5 33.3 %copy-start.3 = (bf16[32,2048]{1,0:T(8,128)(2,1)S(1)}, bf16[32,2048]{1,0:T(8,128)(2,1)}, u32[]{:S(2)}) copy-start(bf16[32,2048]{1,0:T(8,128)(2,1)} %param.21) | copy-start | bytes 393220
  65.7 91.3 %copy-start.2 = (bf16[4,2048]{1,0:T(4,128)(2,1)S(1)}, bf16[4,2048]{1,0:T(4,128)(2,1)}, u32[]{:S(2)}) copy-start(bf16[4,2048]{1,0:T(4,128)(2,1)} %param.17) | copy-start | bytes 49156
  183.2 2.2 copy-start.8
  185.9 6.0 %copy-start.6 = (f32[8,6]{1,0:T(8,128)S(1)}, f32[8,6]{1,0:T(8,128)}, u32[]{:S(2)}) copy-start(f32[8,6]{1,0:T(8,128)} %param.24) | copy-start | bytes 580
  185.9 6.1 %copy-start.10 = (u32[32]{0:T(128)S(1)}, u32[32]{0:T(128)}, u32[]{:S(2)}) copy-start(u32[32]{0:T(128)} %constant.59) | copy-start | bytes 388
  187.8 18.4 %all-to-all-start.2 = ((bf16[16,6,2048]{2,1,0:T(8,128)(2,1)}), bf16[16,6,2048]{2,1,0:T(8,128)(2,1)S(1)}, u32[]{:S(2)}, u32[]{:S(2)}) async-start(bf16[16,6,2048]{2,1,0:T(8,128)(2,1)} %copy.37), calls=%async_computation.2 | async-start | bytes 1048576 | tf_op jit(solution)/shard_map/all_to_all | solution.py:122
Sparse Core Ops, SparseCore 0:
  69.0 87.9 all-reduce.4
where the time goes:
time: 224 us; the launch traced here: 223 us
  waiting for transfers between devices  99.8 us (45%)
  blocking collectives  74.4 us (33%)
  between operations  15.6 us (7%)
  matrix products  12.3 us (5%)
  starting transfers between devices  11.6 us (5%)
  other arithmetic  5.19 us (2%)
  local copies, waits for them, and re-layouts  4.47 us (2%)
    unnamed x2, waiting for transfers between devices  87 us
    psum x1, blocking collectives, local(): adapter_down_rows = lax.psum(adapter_output, 'expert')  30 us
    unnamed x2, blocking collectives  20.7 us
    all_to_all x1, blocking collectives, local(): lax.all_to_all(outgoing, 'expert', split_axis=0, concat_axis=0, tiled=True)  19.2 us
    all_to_all x1, waiting for transfers between devices, local(): lax.all_to_all(partial_value.astype(jnp.bfloat16), 'expert', split_axis=0...  12.8 us
    all_to_all x1, starting transfers between devices, local(): lax.all_to_all(latent_out, 'expert', split_axis=1, concat_axis=0, tiled=T...  7.41 us
  transfers between devices with their start and end apart: 3, of which 2 were waited for; matrix products, arithmetic and copies ran while one was open for 1% of the time, Pallas kernels for 0%

commit v1 on v0

--- a/solution.py
+++ b/solution.py
@@ -70,7 +70,7 @@
     adapter_output = jnp.sum(
         jnp.where(chosen_adapters[:, :, None], down_projected_rows, 0.0), axis=1
     )
-    adapter_down_rows = lax.psum(adapter_output, "expert")
+    adapter_down_rows = jnp.sum(lax.all_gather(adapter_output, "expert"), 0)
     adapter_scaled_output = (ADAPTER_SCALE * adapter_down_rows).astype(jnp.bfloat16)
     first_owned = lax.axis_index("expert") * owned_count
     holder_mask = (

time: 224 us -> 213 us (0.951)
  blocking collectives: 74.4 us -> 62.7 us
    psum x1 -> x0, blocking collectives: 30 us -> none  [local(): adapter_down_rows = lax.psum(adapter_output, 'expert')]
    all_gather x0 -> x1, blocking collectives: none -> 18.3 us  [local(): adapter_down_rows = jnp.sum(lax.all_gather(adapter_output, 'expert'), 0)]
where the time goes in v1:
time: 213 us; the launch traced here: 212 us
  waiting for transfers between devices  100 us (47%)
  blocking collectives  62.7 us (29%)
  between operations  15.6 us (7%)
  matrix products  12.3 us (6%)
  starting transfers between devices  11.6 us (5%)
  other arithmetic  5.22 us (2%)
  local copies, waits for them, and re-layouts  4.47 us (2%)
    unnamed x2, waiting for transfers between devices  87.7 us
    unnamed x2, blocking collectives  20.7 us
    all_to_all x1, blocking collectives, local(): lax.all_to_all(outgoing, 'expert', split_axis=0, concat_axis=0, tiled=True)  19.2 us
    all_gather x1, blocking collectives, local(): adapter_down_rows = jnp.sum(lax.all_gather(adapter_output, 'expert'), 0)  18.3 us
    all_to_all x1, waiting for transfers between devices, local(): lax.all_to_all(partial_value.astype(jnp.bfloat16), 'expert', split_axis=0...  12.8 us
    all_to_all x1, starting transfers between devices, local(): lax.all_to_all(latent_out, 'expert', split_axis=1, concat_axis=0, tiled=T...  7.41 us
    all_gather x1, blocking collectives, local(): column = lax.all_gather(normed, 'dp', axis=0, tiled=True)  4.41 us
  transfers between devices with their start and end apart: 3, of which 2 were waited for; matrix products, arithmetic and copies ran while one was open for 1% of the time, Pallas kernels for 0%

profile of v1, /device:TPU:0, one launch (start us, length us, event | category | flops | bytes accessed | tf_op | source)
XLA Modules:
  0.0 212.4 jit_solution(792038676736914571)
XLA Ops:
  6.5 0.9 iota_compare_fusion.4
  7.4 2.1 %fusion.17 = f32[4,16,512]{2,1,0:T(8,128)S(1)} fusion(bf16[4,16,576]{2,1,0:T(8,128)(2,1)} %param.14, bf16[4,512,576]{1,2,0:T(8,128)(2,1)} %param.15, pred[4,512]{1,0:T(4,128)(4,1)S(1)} %iota_compare_fusion.4), kind=kOutput, calls=%fused_computation.19 | convolution fusion | flops 37814272 | bytes 2566144 | tf_op jit(solution)/shard_map/vmap()/dot_general | solution.py:15
  9.8 2.3 %fusion.19 = bf16[4,16,512]{2,1,0:T(8,128)(2,1)S(1)} fusion(bf16[4,512,576]{1,2,0:T(8,128)(2,1)} %param.15, f32[4,16]{1,0:T(4,128)S(1)} %fusion.31, f32[4,16,512]{2,1,0:T(8,128)S(1)} %fusion.17), kind=kOutput, calls=%fused_computation.21 | convolution fusion | flops 33686080 | bytes 2426880 | tf_op jit(solution)/shard_map/vmap()/dot_general | solution.py:25
  12.1 0.7 copy.29
  12.8 7.4 %all-to-all-start = ((bf16[4,16,512]{2,0,1:T(4,128)(2,1)}), bf16[4,16,512]{2,0,1:T(4,128)(2,1)S(1)}, u32[]{:S(2)}, u32[]{:S(2)}) async-start(bf16[4,16,512]{2,0,1:T(4,128)(2,1)} %copy.29), calls=%async_computation | async-start | bytes 131072 | tf_op jit(solution)/shard_map/all_to_all | solution.py:61
  20.4 0.6 fusion.30
  21.9 12.4 %all-reduce = s32[64]{0:T(128)S(1)} all-reduce(s32[64]{0:T(128)S(1)} %dynamic-update-slice), channel_id=1, replica_groups=mesh['dp'=2,'expert'=16] {'expert'}, use_global_device_ids=true, to_apply=%add | all-reduce | flops 64 | bytes 512
  35.7 18.3 %all-gather.1 = f32[16,64,16]{1,2,0:T(8,128)S(1)} all-gather(f32[1,64,16]{1,2,0:T(8,128)S(1)} %bitcast.47), channel_id=2, replica_groups=mesh['dp'=2,'expert'=16] {'expert'}, dimensions={0}, use_global_device_ids=true | all-gather | bytes 69632 | tf_op jit(solution)/shard_map/all_gather | solution.py:73
  54.0 2.1 fusion.32
  56.1 1.1 convolution_add_fusion
  58.3 87.6 %all-reduce.5.cloned.1.call-done = f32[64,2048]{1,0:T(8,128)} async-done(((f32[64,2048]{1,0:T(8,128)}), f32[64,2048]{1,0:T(8,128)}) %all-reduce.5.cloned.1.call-update) | async-done | bytes 524304
  146.0 1.0 multiply_reduce_fusion
  146.9 0.9 fusion.28
  147.9 4.4 %all-gather.2 = bf16[2,4,2048]{2,1,0:T(4,128)(2,1)S(1)} all-gather(bf16[1,4,2048]{2,1,0:T(4,128)(2,1)S(1)} %fusion.28), channel_id=1, replica_groups=mesh['dp'=2,'expert'=16] {'dp'}, dimensions={0}, use_global_device_ids=true | all-gather | bytes 49152 | tf_op jit(solution)/shard_map/all_gather | solution.py:94
  152.7 19.2 %all_to_all.26 = bf16[16,6,2048]{2,1,0:T(8,128)(2,1)S(1)} all-to-all(bf16[16,6,2048]{2,1,0:T(8,128)(2,1)S(1)} %reshape.125), channel_id=1, replica_groups=mesh['dp'=2,'expert'=16] {'expert'}, dimensions={0} | all-to-all | bytes 786432 | tf_op jit(solution)/shard_map/all_to_all | solution.py:119
  172.1 2.2 %fusion.5 = f32[96,512]{1,0:T(8,128)S(1)} fusion(bf16[96,2048]{1,0:T(8,128)(2,1)S(1)} %reshape.126, bf16[1,2048,512]{2,1,0:T(8,128)(2,1)} %param.25), kind=kOutput, calls=%fused_computation.9 | convolution fusion | flops 201326592 | bytes 2686976 | tf_op jit(solution)/shard_map/dot_general | solution.py:31
  174.9 0.8 convolution_convert_fusion
  175.7 1.0 copy.37
  176.7 4.2 %all-to-all-start.2 = ((bf16[16,6,2048]{2,1,0:T(8,128)(2,1)}), bf16[16,6,2048]{2,1,0:T(8,128)(2,1)S(1)}, u32[]{:S(2)}, u32[]{:S(2)}) async-start(bf16[16,6,2048]{2,1,0:T(8,128)(2,1)} %copy.37), calls=%async_computation.2 | async-start | bytes 1048576 | tf_op jit(solution)/shard_map/all_to_all | solution.py:122
  181.0 0.6 dynamic-slice.3
  182.3 12.8 %all-to-all-done.2 = bf16[16,6,2048]{2,1,0:T(8,128)(2,1)S(1)} async-done(((bf16[16,6,2048]{2,1,0:T(8,128)(2,1)}), bf16[16,6,2048]{2,1,0:T(8,128)(2,1)S(1)}, u32[]{:S(2)}, u32[]{:S(2)}) %all-to-all-start.2) | async-done | bytes 393248 | tf_op jit(solution)/shard_map/all_to_all | solution.py:122
  195.2 0.6 fusion.1
  195.7 8.3 %all-reduce.2 = bf16[8,2048]{1,0:T(8,128)(2,1)S(1)} all-reduce(bf16[8,2048]{1,0:T(8,128)(2,1)S(1)} %fusion.1), channel_id=4, replica_groups=mesh['dp'=2,'expert'=16] {'dp'}, use_global_device_ids=true, to_apply=%region_10.11.clone | all-reduce | flops 16384 | bytes 65536
  204.1 1.5 add_convert_fusion
  (60 shorter events, 3.8 us)
Async XLA Ops:
  6.5 168.3 %copy-start = (bf16[1,2048,512]{2,1,0:T(8,128)(2,1)S(1)}, bf16[1,2048,512]{2,1,0:T(8,128)(2,1)}, u32[]{:S(2)}) copy-start(bf16[1,2048,512]{2,1,0:T(8,128)(2,1)} %param.27) | copy-start | bytes 6291460
  9.6 10.7 %copy-start.4 = (s32[8,6]{1,0:T(8,128)S(1)}, s32[8,6]{1,0:T(8,128)}, u32[]{:S(2)}) copy-start(s32[8,6]{1,0:T(8,128)} %param.23) | copy-start | bytes 580
  9.6 10.8 %copy-start.7 = (u32[32]{0:T(128)S(1)}, u32[32]{0:T(128)}, u32[]{:S(2)}) copy-start(u32[32]{0:T(128)} %constant.49) | copy-start | bytes 388
  9.6 12.1 %copy-start.9 = (s32[4]{0:T(128)S(1)}, s32[4]{0:T(128)}, u32[]{:S(2)}) copy-start(s32[4]{0:T(128)} %param.18) | copy-start | bytes 52
  9.6 24.7 %copy-start.1 = (bf16[512,512]{1,0:T(8,128)(2,1)S(1)}, bf16[512,512]{1,0:T(8,128)(2,1)}, u32[]{:S(2)}) copy-start(bf16[512,512]{1,0:T(8,128)(2,1)} %param.20) | copy-start | bytes 1572868
  9.6 24.9 %copy-start.5 = (bf16[2048]{0:T(1024)(128)(2,1)S(1)}, bf16[2048]{0:T(1024)(128)(2,1)}, u32[]{:S(2)}) copy-start(bf16[2048]{0:T(1024)(128)(2,1)} %param.22) | copy-start | bytes 12292
  12.8 22.4 %all-to-all-start = ((bf16[4,16,512]{2,0,1:T(4,128)(2,1)}), bf16[4,16,512]{2,0,1:T(4,128)(2,1)S(1)}, u32[]{:S(2)}, u32[]{:S(2)}) async-start(bf16[4,16,512]{2,0,1:T(4,128)(2,1)} %copy.29), calls=%async_computation | async-start | bytes 131072 | tf_op jit(solution)/shard_map/all_to_all | solution.py:61
  20.2 125.8 %all-reduce.5.cloned.1.call-start = ((), (), s32[]{:S(2)}) async-start(), calls=%async_computation.3 | async-start | bytes 1048576
  35.1 21.1 %copy-start.3 = (bf16[32,2048]{1,0:T(8,128)(2,1)S(1)}, bf16[32,2048]{1,0:T(8,128)(2,1)}, u32[]{:S(2)}) copy-start(bf16[32,2048]{1,0:T(8,128)(2,1)} %param.21) | copy-start | bytes 393220
  54.0 91.9 %copy-start.2 = (bf16[4,2048]{1,0:T(4,128)(2,1)S(1)}, bf16[4,2048]{1,0:T(4,128)(2,1)}, u32[]{:S(2)}) copy-start(bf16[4,2048]{1,0:T(4,128)(2,1)} %param.17) | copy-start | bytes 49156
  172.1 2.2 %copy-start.8 = (bf16[1,2048,512]{2,1,0:T(8,128)(2,1)S(1)}, bf16[1,2048,512]{2,1,0:T(8,128)(2,1)}, u32[]{:S(2)}) copy-start(bf16[1,2048,512]{2,1,0:T(8,128)(2,1)} %param.26) | copy-start | bytes 6291460
  174.9 6.0 %copy-start.6 = (f32[8,6]{1,0:T(8,128)S(1)}, f32[8,6]{1,0:T(8,128)}, u32[]{:S(2)}) copy-start(f32[8,6]{1,0:T(8,128)} %param.24) | copy-start | bytes 580
  174.9 6.1 %copy-start.10 = (u32[32]{0:T(128)S(1)}, u32[32]{0:T(128)}, u32[]{:S(2)}) copy-start(u32[32]{0:T(128)} %constant.59) | copy-start | bytes 388
  176.7 18.4 %all-to-all-start.2 = ((bf16[16,6,2048]{2,1,0:T(8,128)(2,1)}), bf16[16,6,2048]{2,1,0:T(8,128)(2,1)S(1)}, u32[]{:S(2)}, u32[]{:S(2)}) async-start(bf16[16,6,2048]{2,1,0:T(8,128)(2,1)} %copy.37), calls=%async_computation.2 | async-start | bytes 1048576 | tf_op jit(solution)/shard_map/all_to_all | solution.py:122
Sparse Core Ops, SparseCore 0:
  57.3 88.5 all-reduce.4
